TPU v7x, 32 devices: a whole 2x2x4 slice. The times are simulated.
32 devices in a mesh: sector: 8 (over z, core), term: 4 (over y, x).
Axes of the slice: x: 2, y: 2, z: 4, core: 2. Of those that a mesh axis runs over, the one named last changes fastest.
Arguments:
- psi: bfloat16 [128, 256, 256], P('sector'), may hold values from -6 to 6
- sector_sizes: int32 [128], P('sector'), may hold values from 64 to 256, as said below
- left_env: bfloat16 [192, 8, 256, 256], P('term', 'sector'), may hold values from -0.109375 to 0.109375
- right_env: bfloat16 [192, 8, 256, 256], P('term', 'sector'), may hold values from -0.375 to 0.375
- target: int32 [192, 8], P('term', 'sector'), may hold values from 0 to 127, as said below
- source: int32 [192, 8], P('term', 'sector'), may hold values from 0 to 127, as said below
- live_count: int32 [4, 8], P('term', 'sector'), may hold values from 1 to 48, as said below
Outputs:
- sigma: float32 [128, 256, 256], P('sector', 'term')
Inputs may be any that keep to these rules, and one draw needn't show every extreme that they name: target[j, g] lies among the sectors of sector group g, from g * 16 to (g + 1) * 16 - 1. source[j, g] differs from target[j, g] by at most 16. `live_count`: some device has all 48 slots live in every draw. `sector_sizes`: some sector has all 256 rows live in every draw.
All inputs are finite; a program needn't handle non-finite values.
Results may differ from a plain program's by a relative error of at most 0.0042.
Values may be sent and summed in bfloat16 or wider, within the bound.
A program may use at most 128 MiB of HBM per device.

v0:
```python
import jax
import jax.numpy as jnp
from jax import lax
from jax.sharding import PartitionSpec as P


def extended(x, sides, width):
    for axis, dim in sides:
        devices, length = (lax.axis_size(axis), x.shape[dim])
        up = [(i, (i + 1) % devices) for i in range(devices - 1)]
        down = [(j, i) for i, j in up]
        last = lax.slice_in_dim(x, length - width, length, axis=dim)
        leading = lax.slice_in_dim(x, 0, width, axis=dim)
        before = lax.ppermute(last, axis, up)
        after = lax.ppermute(leading, axis, down)
        x = jnp.concatenate([before, x, after], axis=dim)
    return x


def on_device(psi, sector_sizes, left_env, right_env, target, source, live_count):
    sec_count = psi.shape[0]
    block = psi.shape[1]
    slot_count = left_env.shape[0]
    group = lax.axis_index("sector")
    index_row = jnp.arange(block, dtype=jnp.int32)
    keep = (index_row[None, :, None] < sector_sizes[:, None, None]) & (
        index_row[None, None, :] < sector_sizes[:, None, None]
    )
    masked = jnp.where(keep, psi, jnp.zeros_like(psi))
    left = left_env[:, 0]
    right = right_env[:, 0]
    tgt = target[:, 0]
    src = source[:, 0]
    nearby = extended(masked, (("sector", 0),), sec_count)
    local_src = src - (group * sec_count - sec_count)
    picked = jnp.take(nearby, local_src, axis=0)
    inner = jnp.einsum("jab,jbc->jac", left, picked, preferred_element_type=jnp.float32).astype(
        jnp.bfloat16
    )
    contribution = jnp.einsum("jac,jdc->jad", inner, right, preferred_element_type=jnp.float32)
    alive = (jnp.arange(slot_count, dtype=jnp.int32) < live_count[0, 0]).astype(jnp.float32)
    selector = (
        (tgt - group * sec_count)[:, None] == jnp.arange(sec_count, dtype=jnp.int32)[None, :]
    ).astype(jnp.float32)
    selector = selector * alive[:, None]
    partial_sums = jnp.einsum(
        "js,jad->sad", selector, contribution, precision=lax.Precision.HIGHEST
    )
    partial_sums = jnp.where(keep, partial_sums, jnp.zeros_like(partial_sums))
    return lax.psum_scatter(partial_sums, "term", scatter_dimension=1, tiled=True)


def solution(mesh):
    placed = (
        P("sector", None, None),
        P("sector"),
        P("term", "sector", None, None),
        P("term", "sector", None, None),
        P("term", "sector"),
        P("term", "sector"),
        P("term", "sector"),
    )
    return jax.shard_map(
        on_device, mesh=mesh, in_specs=placed, out_specs=P("sector", "term", None), check_vma=False
    )
```

profile of v0, /device:TPU:9, one launch (start us, length us, event | category | flops | bytes accessed | tf_op | source)
XLA Modules:
  0.0 152.6 jit_solution(1320851909726862016)
XLA Ops:
  6.5 0.0 reduce-scatter.2.cloned.1.call-start
  6.5 0.7 iota_compare_fusion
  7.3 0.1 copy.11
  7.4 6.2 %and_select_fusion.1 = bf16[16,256,256]{2,0,1:T(8,128)(2,1)S(1)} fusion(bf16[16,256,256]{2,1,0:T(8,128)(2,1)} %param.7, pred[16,256]{1,0:T(8,128)(4,1)S(1)} %iota_compare_fusion, pred[16,256]{0,1:T(8,128)(4,1)S(1)} %copy.11), kind=kLoop, calls=%fused_computation.12 | loop fusion | flops 2097152 | bytes 4202496 | tf_op jit(solution)/shard_map/jit(_where)/select_n | solution.py:29
  13.6 3.8 %collective-permute-start = (bf16[16,256,256]{2,0,1:T(8,128)(2,1)S(1)}, bf16[16,256,256]{2,0,1:T(8,128)(2,1)}, u32[]{:S(2)}, u32[]{:S(2)}) collective-permute-start(bf16[16,256,256]{2,0,1:T(8,128)(2,1)S(1)} %and_select_fusion.1), channel_id=1, source_target_pairs={{0,4},{4,8},{8,12},{12,16},{16,20},{20,24},{24,28},{1,5},{5,9},{9,... | collective-permute-start | bytes 6291464 | tf_op jit(solution)/shard_map/ppermute | solution.py:14
  17.4 1.9 %collective-permute-start.1 = (bf16[16,256,256]{2,0,1:T(8,128)(2,1)S(1)}, bf16[16,256,256]{2,0,1:T(8,128)(2,1)}, u32[]{:S(2)}, u32[]{:S(2)}) collective-permute-start(bf16[16,256,256]{2,0,1:T(8,128)(2,1)S(1)} %and_select_fusion.1), channel_id=1, source_target_pairs={{4,0},{8,4},{12,8},{16,12},{20,16},{24,20},{28,24},{5,1},{9,5},{13... | collective-permute-start | bytes 6291464 | tf_op jit(solution)/shard_map/ppermute | solution.py:15
  20.0 0.7 and_bitcast_fusion
  20.7 0.7 subtract_bitcast_fusion
  21.3 19.0 %collective-permute-done = bf16[16,256,256]{2,0,1:T(8,128)(2,1)} collective-permute-done((bf16[16,256,256]{2,0,1:T(8,128)(2,1)S(1)}, bf16[16,256,256]{2,0,1:T(8,128)(2,1)}, u32[]{:S(2)}, u32[]{:S(2)}) %collective-permute-start) | collective-permute-done | bytes 2097184 | tf_op jit(solution)/shard_map/ppermute | solution.py:14
  40.3 4.5 %collective-permute-done.1 = bf16[16,256,256]{2,0,1:T(8,128)(2,1)} collective-permute-done((bf16[16,256,256]{2,0,1:T(8,128)(2,1)S(1)}, bf16[16,256,256]{2,0,1:T(8,128)(2,1)}, u32[]{:S(2)}, u32[]{:S(2)}) %collective-permute-start.1) | collective-permute-done | bytes 2097184 | tf_op jit(solution)/shard_map/ppermute | solution.py:15
  44.8 3.0 %pad_maximum_fusion = bf16[48,256,256]{2,0,1:T(8,128)(2,1)S(1)} fusion(bf16[16,256,256]{2,0,1:T(8,128)(2,1)} %collective-permute-done.1, bf16[16,256,256]{2,0,1:T(8,128)(2,1)S(1)} %and_select_fusion.1, bf16[16,256,256]{2,0,1:T(8,128)(2,1)} %collective-permute-done), kind=kLoop, calls=%fused_computation.3 | loop fusion | flops 18874368 | bytes 12582912 | tf_op jit(solution)/shard_map/concatenate | solution.py:16
  47.9 4.9 %copy.13 = bf16[48,256,256]{2,1,0:T(8,128)(2,1)} copy(bf16[48,256,256]{2,0,1:T(8,128)(2,1)S(1)} %pad_maximum_fusion) | data formatting | bytes 12582912 | tf_op jit(solution)/shard_map/concatenate | solution.py:16
  52.8 7.7 %gather_fusion = bf16[48,256,256]{2,1,0:T(8,128)(2,1)} fusion(bf16[48,256,256]{2,1,0:T(8,128)(2,1)} %copy.13, s32[1024]{0:T(1024)S(1)} %pad_clamp_fusion), kind=kCustom, calls=%fused_computation | custom fusion | bytes 12583104 | tf_op jit(solution)/shard_map/jit(_take)/gather | solution.py:36
  60.5 11.1 %fusion.2 = f32[48,256,256]{2,1,0:T(8,128)} fusion(bf16[48,1,256,256]{3,2,1,0:T(8,128)(2,1)} %param.10, bf16[48,1,256,256]{3,2,1,0:T(8,128)(2,1)} %param.9, bf16[48,256,256]{2,1,0:T(8,128)(2,1)} %gather_fusion, pred[48]{0:T(512)(128)(4,1)S(1)} %get-tuple-element.5), kind=kOutput, calls=%fused_computation.4 | convolution fusion | flops 3227516928 | bytes 31457328 | tf_op jit(solution)/shard_map/jac,jdc->jad/dot_general | solution.py:40
  71.5 19.2 %and_select_fusion = f32[16,256,256]{2,0,1:T(8,128)} fusion(pred[16,256]{1,0:T(8,128)(4,1)S(1)} %iota_compare_fusion, pred[16,256]{0,1:T(8,128)(4,1)S(1)} %copy.11, f32[48,256,256]{2,1,0:T(8,128)} %fusion.2, f32[48]{0:T(128)S(1)} %compare_convert_fusion, s32[48]{0:T(128)S(1)} %subtract_bitcast_fusion), kind=kOutput, calls=%fused_computation.11 | convolution fusion | flops 606078464 | bytes 16785792 | tf_op jit(solution)/shard_map/js,jad->sad/dot_general | solution.py:46
  90.7 0.0 reduce-scatter.2.cloned.1.call-update
  90.7 52.2 %reduce-scatter.2.cloned.1.call-done = f32[16,64,256]{2,0,1:T(8,128)} async-done(((f32[16,256,256]{2,0,1:T(8,128)}), f32[16,64,256]{2,0,1:T(8,128)}) %reduce-scatter.2.cloned.1.call-update) | async-done | bytes 1048592 | tf_op jit(solution)/shard_map/reduce_scatter | solution.py:50
  143.0 2.8 %copy.14 = f32[16,64,256]{2,1,0:T(8,128)} copy(f32[16,64,256]{2,0,1:T(8,128)} %reduce-scatter.2.cloned.1.call-done) | data formatting | bytes 2097152 | tf_op jit(solution)/shard_map/reduce_scatter | solution.py:50
  (2 shorter events, 0.0 us)
Async XLA Ops:
  6.5 136.4 %reduce-scatter.2.cloned.1.call-start = ((), (), s32[]{:S(2)}) async-start(), calls=%async_computation.1 | async-start | bytes 5242880 | tf_op jit(solution)/shard_map/reduce_scatter | solution.py:50
  13.6 26.7 %collective-permute-start = (bf16[16,256,256]{2,0,1:T(8,128)(2,1)S(1)}, bf16[16,256,256]{2,0,1:T(8,128)(2,1)}, u32[]{:S(2)}, u32[]{:S(2)}) collective-permute-start(bf16[16,256,256]{2,0,1:T(8,128)(2,1)S(1)} %and_select_fusion.1), channel_id=1, source_target_pairs={{0,4},{4,8},{8,12},{12,16},{16,20},{20,24},{24,28},{1,5},{5,9},{9,... | collective-permute-start | bytes 6291464 | tf_op jit(solution)/shard_map/ppermute | solution.py:14
  17.4 27.5 %collective-permute-start.1 = (bf16[16,256,256]{2,0,1:T(8,128)(2,1)S(1)}, bf16[16,256,256]{2,0,1:T(8,128)(2,1)}, u32[]{:S(2)}, u32[]{:S(2)}) collective-permute-start(bf16[16,256,256]{2,0,1:T(8,128)(2,1)S(1)} %and_select_fusion.1), channel_id=1, source_target_pairs={{4,0},{8,4},{12,8},{16,12},{20,16},{24,20},{28,24},{5,1},{9,5},{13... | collective-permute-start | bytes 6291464 | tf_op jit(solution)/shard_map/ppermute | solution.py:15
Sparse Core Ops, SparseCore 0:
  90.8 52.0 reduce-scatter.1
where the time goes:
time: 155 us; the launch traced here: 153 us
  waiting for transfers between devices  75.8 us (49%)
  matrix products  30.2 us (19%)
  local copies, waits for them, and re-layouts  15.5 us (10%)
  between operations  14.1 us (9%)
  other arithmetic  11.3 us (7%)
  starting transfers between devices  5.69 us (4%)
    reduce_scatter x1, waiting for transfers between devices, on_device(): lax.psum_scatter(partial_sums, 'term', scatter_dimension=1, tiled=True)  52.2 us
    dot_general x1, matrix products, on_device(): jnp.einsum('js,jad->sad', selector, contribution, precision=lax.Precision...  19.2 us
    ppermute x1, waiting for transfers between devices, extended(): before = lax.ppermute(last, axis, up)  19 us
    dot_general x1, matrix products, on_device(): jnp.einsum('jac,jdc->jad', inner, right, preferred_element_type=jnp.float32)  11.1 us
    gather x1, local copies, waits for them, and re-layouts, on_device(): picked = jnp.take(nearby, local_src, axis=0)  7.68 us
    select_n x1, other arithmetic, on_device(): masked = jnp.where(keep, psi, jnp.zeros_like(psi))  6.21 us
    concatenate x1, local copies, waits for them, and re-layouts, extended(): x = jnp.concatenate([before, x, after], axis=dim)  4.9 us
    ppermute x1, waiting for transfers between devices, extended(): after = lax.ppermute(leading, axis, down)  4.5 us
  transfers between devices with their start and end apart: 3, of which 3 were waited for; matrix products, arithmetic and copies ran while one was open for 1% of the time, Pallas kernels for 0%

commit v1 on v0

v1 whole, which is shorter than its diff:
```python
import functools
import math

import jax
import jax.numpy as jnp
from jax import lax
from jax.experimental import pallas as pl
from jax.experimental.pallas import tpu as pltpu
from jax.sharding import PartitionSpec as P

MESH = pl.DeviceIdType.MESH
RS_GROUPS = 4
UNROLL = 4


def kernel(
    terms, groups,
    order_ref, ends_ref, sizes_ref, psi_ref, left_ref, right_ref,
    out_ref,
    nearby, left, right, running, outgoing, incoming, own,
    load_sems, near_send, near_recv, far_send, far_recv, pass_send, pass_recv, sum_send, sum_recv,
):
    secs, block = psi_ref.shape[0], psi_ref.shape[1]
    slots = left_ref.shape[0]
    rows = block // terms
    side = math.isqrt(terms)
    quarter = secs // 4
    group, term = lax.axis_index("sector"), lax.axis_index("term")
    odd = lax.rem(group, 2)
    near = group + 1 - 2 * odd
    far = group - 1 + 2 * odd
    has_far = jnp.logical_and(far >= 0, far < groups)
    col, row = lax.rem(term, side), lax.div(term, side)
    odd_col, odd_row = lax.rem(col, 2), lax.rem(row, 2)
    col_mate = term + 1 - 2 * odd_col
    row_mate = term + (1 - 2 * odd_row) * side

    psi_load = pltpu.make_async_copy(psi_ref, nearby.at[pl.ds(0, secs)], load_sems.at[0])
    left_load = pltpu.make_async_copy(left_ref, left, load_sems.at[1])
    right_load = pltpu.make_async_copy(right_ref, right, load_sems.at[2])
    psi_load.start()
    left_load.start()
    right_load.start()

    barrier = pltpu.get_barrier_semaphore()
    pl.semaphore_signal(barrier, inc=1, device_id={"sector": near}, device_id_type=MESH)
    for d in range(1, terms):
        pl.semaphore_signal(
            barrier, inc=1, device_id={"term": lax.rem(term + d, terms)}, device_id_type=MESH
        )

    @pl.when(has_far)
    def _():
        pl.semaphore_signal(barrier, inc=1, device_id={"sector": far}, device_id_type=MESH)

    psi_load.wait()
    index_row = lax.broadcasted_iota(jnp.int32, (block, block), 0)
    index_col = lax.broadcasted_iota(jnp.int32, (block, block), 1)
    reach = jnp.maximum(index_row, index_col)

    def mask(q, carry):
        nearby[q] = jnp.where(reach < sizes_ref[q], nearby[q], jnp.zeros((block, block), nearby.dtype))
        return carry

    lax.fori_loop(0, secs, mask, 0)
    pl.semaphore_wait(barrier, terms + has_far.astype(jnp.int32))

    near_copy = pltpu.make_async_remote_copy(
        nearby.at[pl.ds(0, secs)], nearby.at[pl.ds(secs, secs)], near_send, near_recv,
        device_id={"sector": near}, device_id_type=MESH,
    )

    def piece(i, mine):
        along_row, k = i % 2, i // 2
        odd_here = odd_row if along_row else odd_col
        if not mine:
            odd_here = 1 - odd_here
        return 2 * quarter * along_row + odd_here * quarter + k

    pieces = 2 * quarter

    def far_copy(i):
        q = piece(i, True)
        return pltpu.make_async_remote_copy(
            nearby.at[q], nearby.at[2 * secs + q], far_send.at[i], far_recv.at[i],
            device_id={"sector": far}, device_id_type=MESH,
        )

    def pass_copy(i, mine=True):
        q = piece(i, mine)
        return pltpu.make_async_remote_copy(
            nearby.at[2 * secs + q], nearby.at[2 * secs + q], pass_send.at[i], pass_recv.at[i],
            device_id={"term": row_mate if i % 2 else col_mate}, device_id_type=MESH,
        )

    @pl.when(has_far)
    def _():
        for i in range(pieces):
            far_copy(i).start()

    near_copy.start()

    @pl.when(has_far)
    def _():
        for i in range(pieces):
            far_copy(i).wait_recv()
            pass_copy(i).start()

    left_load.wait()
    right_load.wait()
    near_copy.wait()

    @pl.when(has_far)
    def _():
        for i in range(pieces):
            pass_copy(i, False).wait_recv()
        for i in range(pieces):
            far_copy(i).wait_send()
            pass_copy(i).wait_send()

    def visit(step, carry):
        for u in range(UNROLL):
            k = step * UNROLL + u
            code = order_ref[k]
            slot, src, tgt = code & 255, (code >> 8) & 255, code >> 16
            before = jnp.maximum(k - 1, 0)
            again = jnp.logical_and(k > 0, (order_ref[before] >> 16) == tgt)
            inner = jnp.dot(left[slot], nearby[src], preferred_element_type=jnp.float32).astype(
                jnp.bfloat16
            )
            here = lax.dot_general(
                inner, right[slot], (((1,), (1,)), ((), ())), preferred_element_type=jnp.float32
            )
            so_far = running[before]
            running[k] = here + jnp.where(again, so_far, jnp.zeros_like(so_far))
        return carry

    lax.fori_loop(0, slots // UNROLL, visit, 0)

    span = secs // RS_GROUPS

    def sum_copy(d, g):
        peer = lax.rem(term + d, terms)
        return pltpu.make_async_remote_copy(
            outgoing.at[peer, pl.ds(g * span, span)], incoming.at[d - 1, pl.ds(g * span, span)],
            sum_send.at[d - 1, g], sum_recv.at[d - 1, g],
            device_id={"term": peer}, device_id_type=MESH,
        )

    for g in range(RS_GROUPS):
        def finish(q, carry):
            end = ends_ref[q]
            start = jnp.where(q > 0, ends_ref[jnp.maximum(q - 1, 0)], 0)
            some = end > start
            at = jnp.maximum(end - 1, 0)
            for t in range(terms):
                total = running[at, t * rows : (t + 1) * rows, :]
                outgoing[t, q] = jnp.where(some, total, jnp.zeros_like(total)).astype(outgoing.dtype)
            total = running[at, pl.ds(pl.multiple_of(term * rows, rows), rows), :]
            own[q] = jnp.where(some, total, jnp.zeros_like(total))
            return carry

        lax.fori_loop(g * span, (g + 1) * span, finish, 0)
        for d in range(1, terms):
            sum_copy(d, g).start()

    for g in range(RS_GROUPS):
        for d in range(1, terms):
            sum_copy(d, g).wait_recv()

        def add(q, carry):
            total = own[q]
            for d in range(1, terms):
                total = total + incoming[d - 1, q].astype(jnp.float32)
            out_ref[q] = total
            return carry

        lax.fori_loop(g * span, (g + 1) * span, add, 0)
    for g in range(RS_GROUPS):
        for d in range(1, terms):
            sum_copy(d, g).wait_send()


def on_device(terms, groups, psi, sector_sizes, left_env, right_env, target, source, live_count):
    secs, block = psi.shape[0], psi.shape[1]
    slots = left_env.shape[0]
    rows = block // terms
    group = lax.axis_index("sector")
    tgt = target[:, 0] - group * secs
    src_group = source[:, 0] // secs
    place = jnp.where(src_group == group, 0, jnp.where(src_group == group + 1 - 2 * (group % 2), 1, 2))
    src = source[:, 0] - src_group * secs + place * secs
    slot = jnp.arange(slots, dtype=jnp.int32)
    tgt = jnp.where(slot < live_count[0, 0], tgt, secs)
    key = tgt * slots + slot
    rank = jnp.sum((key[None, :] < key[:, None]).astype(jnp.int32), axis=1)
    code = slot + src * 256 + tgt * 65536
    order = jnp.sum(jnp.where(rank[None, :] == slot[:, None], code[None, :], 0), axis=1)
    sec = jnp.arange(secs, dtype=jnp.int32)
    ends = jnp.sum((tgt[None, :] <= sec[:, None]).astype(jnp.int32), axis=1)
    pieces = 2 * (secs // 4)
    dma = pltpu.SemaphoreType.DMA
    total = pl.pallas_call(
        functools.partial(kernel, terms, groups),
        out_shape=jax.ShapeDtypeStruct((secs, rows, block), jnp.float32),
        in_specs=[pl.BlockSpec(memory_space=pltpu.SMEM)] * 3 + [pl.BlockSpec(memory_space=pl.ANY)] * 3,
        out_specs=pl.BlockSpec(memory_space=pltpu.VMEM),
        scratch_shapes=[
            pltpu.VMEM((3 * secs, block, block), jnp.bfloat16),
            pltpu.VMEM((slots, block, block), jnp.bfloat16),
            pltpu.VMEM((slots, block, block), jnp.bfloat16),
            pltpu.VMEM((slots, block, block), jnp.float32),
            pltpu.VMEM((terms, secs, rows, block), jnp.bfloat16),
            pltpu.VMEM((terms - 1, secs, rows, block), jnp.bfloat16),
            pltpu.VMEM((secs, rows, block), jnp.float32),
            dma((3,)), dma, dma, dma((pieces,)), dma((pieces,)), dma((pieces,)), dma((pieces,)),
            dma((terms - 1, RS_GROUPS)), dma((terms - 1, RS_GROUPS)),
        ],
        compiler_params=pltpu.CompilerParams(
            collective_id=0, has_side_effects=True, vmem_limit_bytes=60 * 1024 * 1024
        ),
    )(order, ends, sector_sizes, psi, left_env[:, 0], right_env[:, 0])
    index_row = lax.axis_index("term") * rows + jnp.arange(rows, dtype=jnp.int32)
    index_col = jnp.arange(block, dtype=jnp.int32)
    keep = (index_row[None, :, None] < sector_sizes[:, None, None]) & (
        index_col[None, None, :] < sector_sizes[:, None, None]
    )
    return jnp.where(keep, total, jnp.zeros_like(total))


def solution(mesh):
    placed = (
        P("sector", None, None),
        P("sector"),
        P("term", "sector", None, None),
        P("term", "sector", None, None),
        P("term", "sector"),
        P("term", "sector"),
        P("term", "sector"),
    )
    return jax.shard_map(
        functools.partial(on_device, mesh.shape["term"], mesh.shape["sector"]),
        mesh=mesh, in_specs=placed, out_specs=P("sector", "term", None), check_vma=False,
    )
```

time: 155 us -> 61.3 us (0.40); the launches traced: 153 us -> 61.1 us
  waiting for transfers between devices: 75.8 us -> 0 us
  Pallas kernels: 0 us -> 54.4 us
  matrix products: 30.2 us -> 0 us
  local copies, waits for them, and re-layouts: 15.5 us -> 0.01 us
  between operations: 14.1 us -> 0.68 us
  starting transfers between devices: 5.69 us -> 0 us
  other arithmetic: 11.3 us -> 6.07 us
    pallas_call x0 -> x1, Pallas kernels: none -> 54.4 us  [on_device(): pl.pallas_call(functools.partial(kernel, terms, groups), out_shape=jax.Sh...]
    reduce_scatter x1 -> x0, waiting for transfers between devices: 52.2 us -> none  [on_device(): lax.psum_scatter(partial_sums, 'term', scatter_dimension=1, tiled=True)]
    dot_general x2 -> x0, matrix products: 30.2 us -> none  [the longest x1 19.2 us: on_device(): jnp.einsum('js,jad->sad', selector, contribution, precision=lax.Precision...]
    ppermute x2 -> x0, waiting for transfers between devices: 23.5 us -> none  [the longest x1 19 us: extended(): before = lax.ppermute(last, axis, up)]
    gather x1 -> x0, local copies, waits for them, and re-layouts: 7.68 us -> none  [on_device(): picked = jnp.take(nearby, local_src, axis=0)]
    ppermute x2 -> x0, starting transfers between devices: 5.69 us -> none  [the longest x1 3.77 us: extended(): before = lax.ppermute(last, axis, up)]
    concatenate x1 -> x0, local copies, waits for them, and re-layouts: 4.9 us -> none  [extended(): x = jnp.concatenate([before, x, after], axis=dim)]
    select_n x1, other arithmetic: 6.21 us -> 2.4 us  [on_device(): return jnp.where(keep, total, jnp.zeros_like(total))]
  transfers between devices with their start and end apart: 3 -> 0, of which waited for: 3 -> 0; matrix products, arithmetic and copies ran while one was open for 1% -> 0% of each run, Pallas kernels for 0% -> 0%
where the time goes in v1:
time: 61.3 us; the launch traced here: 61.1 us
  Pallas kernels  54.4 us (89%)
  other arithmetic  6.07 us (10%)
  between operations  0.68 us (1%)
    pallas_call x1, Pallas kernels, on_device(): pl.pallas_call(functools.partial(kernel, terms, groups), out_shape=jax.Sh...  54.4 us
    select_n x1, other arithmetic, on_device(): return jnp.where(keep, total, jnp.zeros_like(total))  2.4 us

profile of v1, /device:TPU:9, one launch (start us, length us, event | category | flops | bytes accessed | tf_op | source)
XLA Modules:
  0.0 61.1 jit_solution(17773894398136200569)
XLA Ops:
  0.7 0.7 %iota_add_fusion = (s32[48]{0:T(128)S(1)}, s32[48]{0:T(128)S(1)}) fusion(s32[48,1]{0,1:T(1,128)} %param.11, s32[]{:T(128)S(6)} %mul.59, s32[]{:T(128)} %bitcast.23), kind=kLoop, calls=%fused_computation.24 | loop fusion | flops 240 | bytes 584 | tf_op jit(solution)/shard_map/add | solution.py:195
  1.3 0.7 %multiply_add_fusion = s32[48]{0:T(128)S(1)} fusion(s32[48]{0:T(128)S(1)} %get-tuple-element.6, s32[48,1]{0,1:T(1,128)} %param.12, s32[]{:T(128)S(6)} %sub.41, s32[]{:T(128)S(6)} %axis_index.25), kind=kLoop, calls=%fused_computation.22 | loop fusion | flops 1296 | bytes 584 | tf_op jit(solution)/shard_map/add | solution.py:197
  2.0 0.7 %fusion.4 = s32[48]{0:T(128)S(1)} fusion(s32[48,1]{0,1:T(1,128)} %param.11, s32[]{:T(128)} %bitcast.24, s32[]{:T(128)S(6)} %mul.59), kind=kLoop, calls=%fused_computation.23 | loop fusion | flops 240 | bytes 392 | tf_op jit(solution)/shard_map/lt | solution.py:196
  2.7 0.2 convert_reduce_fusion
  2.8 0.6 %select_reduce_fusion.order_ref = s32[48]{0:T(128)} fusion(s32[48]{0:T(128)S(1)} %multiply_add_fusion, s32[48]{0:T(128)S(1)} %convert_reduce_fusion), kind=kLoop, calls=%fused_computation.1 | loop fusion | flops 6864 | bytes 576 | tf_op jit(solution)/shard_map/reduce_sum | solution.py:198
  3.5 0.7 %convert_reduce_fusion.1.ends_ref = s32[16]{0:T(128)} fusion(s32[48]{0:T(128)S(1)} %get-tuple-element.6), kind=kLoop, calls=%fused_computation.5 | loop fusion | flops 2288 | bytes 256 | tf_op jit(solution)/shard_map/reduce_sum | solution.py:200
  4.2 0.0 copy-start
  4.2 54.4 %shard_map.73 = f32[16,64,256]{2,1,0:T(8,128)} custom-call(s32[48]{0:T(128)} %select_reduce_fusion.order_ref, s32[16]{0:T(128)} %convert_reduce_fusion.1.ends_ref, s32[16]{0:T(128)} %sizes_ref.1, bf16[16,256,256]{2,1,0:T(8,128)(2,1)} %psi_ref.1, bf16[48,256,256]{2,1,0:T(8,128)(2,1)} %bitcast.25, bf16[48,256,256]{2,1,0:T(8,128)(2,1)} %bitcast.26), custom_call_target="tpu_custom_call" | custom-call | tf_op jit(solution)/shard_map/pallas_call | solution.py:203
  58.6 0.0 copy-done
  58.6 0.1 broadcast_compare_fusion
  58.7 0.1 iota_compare_fusion.1
  58.7 2.4 %and_select_fusion = f32[16,64,256]{2,1,0:T(8,128)} fusion(f32[16,64,256]{2,1,0:T(8,128)} %shard_map.73, pred[16,256]{1,0:T(8,128)(4,1)S(1)} %iota_compare_fusion.1, pred[16,64]{1,0:T(8,128)(4,1)S(1)} %broadcast_compare_fusion), kind=kLoop, calls=%fused_computation | loop fusion | flops 524288 | bytes 2102272 | tf_op jit(solution)/shard_map/jit(_where)/select_n | solution.py:228
  (1 shorter events, 0.0 us)
Async XLA Ops:
  4.2 54.4 %copy-start = (s32[16]{0:T(128)S(1)}, s32[16]{0:T(128)}, u32[]{:S(2)}) copy-start(s32[16]{0:T(128)} %sizes_ref.1) | copy-start | bytes 196

commit v2 on v1

v2 whole, which is shorter than its diff:
```python
import functools
import math

import jax
import jax.numpy as jnp
from jax import lax
from jax.experimental import pallas as pl
from jax.experimental.pallas import tpu as pltpu
from jax.sharding import PartitionSpec as P

MESH = pl.DeviceIdType.MESH
SPLITS = 4
HALVES = 2
UNROLL = 4


def kernel(
    terms, groups,
    live_ref, sizes_ref, target_ref, source_ref, psi_ref, left_ref, right_ref,
    out_ref,
    nearby, left, right, inner, running, first_out, first_in, second_out, second_in, own, table, plan,
    load_sems, near_send, near_recv, far_send, far_recv, pass_send, pass_recv,
    first_send, first_recv, second_send, second_recv,
):
    secs, block = psi_ref.shape[0], psi_ref.shape[1]
    slots = left_ref.shape[0]
    rows = block // terms
    side = math.isqrt(terms)
    quarter = secs // 4
    group, term = lax.axis_index("sector"), lax.axis_index("term")
    odd = lax.rem(group, 2)
    near = group + 1 - 2 * odd
    far = group - 1 + 2 * odd
    has_far = jnp.logical_and(far >= 0, far < groups)
    col, row = lax.rem(term, side), lax.div(term, side)
    odd_col, odd_row = lax.rem(col, 2), lax.rem(row, 2)
    col_mate = term + 1 - 2 * odd_col
    row_mate = term + (1 - 2 * odd_row) * side

    psi_load = pltpu.make_async_copy(psi_ref, nearby.at[pl.ds(0, secs)], load_sems.at[0])
    left_load = pltpu.make_async_copy(left_ref, left, load_sems.at[1])
    right_load = pltpu.make_async_copy(right_ref, right, load_sems.at[2])
    psi_load.start()
    left_load.start()
    right_load.start()

    barrier = pltpu.get_barrier_semaphore()
    pl.semaphore_signal(barrier, inc=1, device_id={"sector": near}, device_id_type=MESH)
    for d in range(1, terms):
        pl.semaphore_signal(
            barrier, inc=1, device_id={"term": lax.rem(term + d, terms)}, device_id_type=MESH
        )

    @pl.when(has_far)
    def _():
        pl.semaphore_signal(barrier, inc=1, device_id={"sector": far}, device_id_type=MESH)

    psi_load.wait()
    index_row = lax.broadcasted_iota(jnp.int32, (block, block), 0)
    index_col = lax.broadcasted_iota(jnp.int32, (block, block), 1)
    reach = jnp.maximum(index_row, index_col)

    def mask(q, carry):
        nearby[q] = jnp.where(reach < sizes_ref[q], nearby[q], jnp.zeros((block, block), nearby.dtype))
        return carry

    lax.fori_loop(0, secs, mask, 0)
    pl.semaphore_wait(barrier, terms + has_far.astype(jnp.int32))

    near_copy = pltpu.make_async_remote_copy(
        nearby.at[pl.ds(0, secs)], nearby.at[pl.ds(secs, secs)], near_send, near_recv,
        device_id={"sector": near}, device_id_type=MESH,
    )

    def piece(i, mine):
        along_row, k = i % 2, i // 2
        odd_here = odd_row if along_row else odd_col
        if not mine:
            odd_here = 1 - odd_here
        return 2 * quarter * along_row + odd_here * quarter + k

    pieces = 2 * quarter

    def far_copy(i):
        q = piece(i, True)
        return pltpu.make_async_remote_copy(
            nearby.at[q], nearby.at[2 * secs + q], far_send.at[i], far_recv.at[i],
            device_id={"sector": far}, device_id_type=MESH,
        )

    def pass_copy(i, mine=True):
        q = piece(i, mine)
        return pltpu.make_async_remote_copy(
            nearby.at[2 * secs + q], nearby.at[2 * secs + q], pass_send.at[i], pass_recv.at[i],
            device_id={"term": row_mate if i % 2 else col_mate}, device_id_type=MESH,
        )

    @pl.when(has_far)
    def _():
        for i in range(pieces):
            far_copy(i).start()

    near_copy.start()

    lane = lax.broadcasted_iota(jnp.int32, (slots, slots), 1)
    line = lax.broadcasted_iota(jnp.int32, (slots, slots), 0)
    slot = lax.broadcasted_iota(jnp.int32, (1, slots), 1)

    def as_column(values):
        return jnp.sum(jnp.where(lane == line, values, 0), axis=1, keepdims=True)

    tgt = jnp.where(slot < live_ref[0, 0], target_ref[...] - group * secs, secs)
    from_own = source_ref[...] - group * secs
    from_near = source_ref[...] - near * secs
    from_far = source_ref[...] - far * secs
    src = jnp.where(
        (from_own >= 0) & (from_own < secs), from_own,
        jnp.where((from_near >= 0) & (from_near < secs), secs + from_near, 2 * secs + jnp.clip(from_far, 0, secs - 1)),
    )
    key = tgt * slots + slot
    rank = jnp.sum((key < as_column(key)).astype(jnp.int32), axis=1, keepdims=True)
    code = as_column(slot + src * 256 + tgt * 65536)
    table[...] = jnp.zeros_like(table)
    table[0:1, 0:slots] = jnp.sum(jnp.where(rank == lane, code, 0), axis=0, keepdims=True)
    sec = lax.broadcasted_iota(jnp.int32, (slots, 128), 1)
    table[1:2, :] = jnp.sum((as_column(tgt) <= sec).astype(jnp.int32), axis=0, keepdims=True)
    plan_load = pltpu.make_async_copy(table, plan, load_sems.at[3])
    plan_load.start()
    plan_load.wait()

    @pl.when(has_far)
    def _():
        for i in range(pieces):
            far_copy(i).wait_recv()
            pass_copy(i).start()

    left_load.wait()
    right_load.wait()
    near_copy.wait()

    @pl.when(has_far)
    def _():
        for i in range(pieces):
            pass_copy(i, False).wait_recv()
        for i in range(pieces):
            far_copy(i).wait_send()
            pass_copy(i).wait_send()

    def multiply(step, carry):
        for u in range(UNROLL):
            k = step * UNROLL + u
            code = plan[0, k]
            inner[k] = jnp.dot(
                left[code & 255], nearby[(code >> 8) & 255], preferred_element_type=jnp.float32
            ).astype(jnp.bfloat16)
        return carry

    lax.fori_loop(0, slots // UNROLL, multiply, 0)

    width = block // HALVES
    span = secs // SPLITS

    def places(part):
        return (row, col) if part % 2 else (col, row)

    def term_at(part, first, second):
        return first * side + second if part % 2 else second * side + first

    def first_copy(half, part, d):
        first, second = places(part)
        to = lax.rem(first + d, side)
        return pltpu.make_async_remote_copy(
            first_out.at[half, part, to], first_in.at[half, part, d - 1],
            first_send.at[half, part, d - 1], first_recv.at[half, part, d - 1],
            device_id={"term": term_at(part, to, second)}, device_id_type=MESH,
        )

    def second_copy(half, part, d):
        first, second = places(part)
        to = lax.rem(second + d, side)
        return pltpu.make_async_remote_copy(
            second_out.at[half, part, d - 1], second_in.at[half, part, d - 1],
            second_send.at[half, part, d - 1], second_recv.at[half, part, d - 1],
            device_id={"term": term_at(part, first, to)}, device_id_type=MESH,
        )

    def summed(half, q, place):
        end = plan[1, q]
        start = jnp.where(q > 0, plan[1, jnp.maximum(q - 1, 0)], 0)
        at = pl.multiple_of(place * rows, rows)
        total = running[half, jnp.maximum(end - 1, 0), pl.ds(at, rows), :]
        return jnp.where(end > start, total, jnp.zeros_like(total))

    for half in range(HALVES):
        def visit(step, carry):
            for u in range(UNROLL):
                k = step * UNROLL + u
                code = plan[0, k]
                before = jnp.maximum(k - 1, 0)
                again = jnp.logical_and(k > 0, (plan[0, before] >> 16) == (code >> 16))
                here = lax.dot_general(
                    inner[k], right[code & 255, half * width : (half + 1) * width, :],
                    (((1,), (1,)), ((), ())), preferred_element_type=jnp.float32,
                )
                so_far = running[half, before]
                running[half, k] = here + jnp.where(again, so_far, jnp.zeros_like(so_far))
            return carry

        lax.fori_loop(0, slots // UNROLL, visit, 0)

        for part in range(SPLITS):
            first, second = places(part)

            def give(i, carry):
                for a in range(side):
                    for b in range(side):
                        first_out[half, part, a, b, i] = summed(
                            half, part * span + i, term_at(part, a, b)
                        ).astype(first_out.dtype)
                return carry

            lax.fori_loop(0, span, give, 0)
            for d in range(1, side):
                first_copy(half, part, d).start()

    for half in range(HALVES):
        for part in range(SPLITS):
            first, second = places(part)
            for d in range(1, side):
                first_copy(half, part, d).wait_recv()

            def pass_on(i, carry):
                def partial_sum(b):
                    total = summed(half, part * span + i, term_at(part, first, b))
                    for d in range(1, side):
                        total = total + first_in[half, part, d - 1, b, i].astype(jnp.float32)
                    return total

                for d in range(1, side):
                    second_out[half, part, d - 1, i] = partial_sum(lax.rem(second + d, side)).astype(
                        second_out.dtype
                    )
                own[half, part * span + i] = partial_sum(second)
                return carry

            lax.fori_loop(0, span, pass_on, 0)
            for d in range(1, side):
                second_copy(half, part, d).start()

    for half in range(HALVES):
        columns = slice(half * width, (half + 1) * width)
        for part in range(SPLITS):
            for d in range(1, side):
                second_copy(half, part, d).wait_recv()

            def add(i, carry):
                total = own[half, part * span + i]
                for d in range(1, side):
                    total = total + second_in[half, part, d - 1, i].astype(jnp.float32)
                out_ref[part * span + i, :, columns] = total
                return carry

            lax.fori_loop(0, span, add, 0)
    for half in range(HALVES):
        for part in range(SPLITS):
            for d in range(1, side):
                first_copy(half, part, d).wait_send()
                second_copy(half, part, d).wait_send()


def on_device(terms, groups, psi, sector_sizes, left_env, right_env, target, source, live_count):
    secs, block = psi.shape[0], psi.shape[1]
    slots = left_env.shape[0]
    rows, side, span, width = block // terms, math.isqrt(terms), secs // SPLITS, block // HALVES
    pieces = 2 * (secs // 4)
    dma = pltpu.SemaphoreType.DMA
    smem, vmem, here = (pl.BlockSpec(memory_space=m) for m in (pltpu.SMEM, pltpu.VMEM, pl.ANY))
    total = pl.pallas_call(
        functools.partial(kernel, terms, groups),
        out_shape=jax.ShapeDtypeStruct((secs, rows, block), jnp.float32),
        in_specs=[smem, smem, vmem, vmem, here, here, here],
        out_specs=vmem,
        scratch_shapes=[
            pltpu.VMEM((3 * secs, block, block), jnp.bfloat16),
            pltpu.VMEM((slots, block, block), jnp.bfloat16),
            pltpu.VMEM((slots, block, block), jnp.bfloat16),
            pltpu.VMEM((slots, block, block), jnp.bfloat16),
            pltpu.VMEM((HALVES, slots, block, width), jnp.float32),
            pltpu.VMEM((HALVES, SPLITS, side, side, span, rows, width), jnp.bfloat16),
            pltpu.VMEM((HALVES, SPLITS, side - 1, side, span, rows, width), jnp.bfloat16),
            pltpu.VMEM((HALVES, SPLITS, side - 1, span, rows, width), jnp.bfloat16),
            pltpu.VMEM((HALVES, SPLITS, side - 1, span, rows, width), jnp.bfloat16),
            pltpu.VMEM((HALVES, secs, rows, width), jnp.float32),
            pltpu.VMEM((8, 128), jnp.int32),
            pltpu.SMEM((8, 128), jnp.int32),
            dma((4,)), dma, dma, dma((pieces,)), dma((pieces,)), dma((pieces,)), dma((pieces,)),
            *[dma((HALVES, SPLITS, side - 1))] * 4,
        ],
        compiler_params=pltpu.CompilerParams(
            collective_id=0, has_side_effects=True, vmem_limit_bytes=54 * 1024 * 1024
        ),
    )(
        live_count, sector_sizes, target.reshape(1, slots), source.reshape(1, slots),
        psi, left_env[:, 0], right_env[:, 0],
    )
    index_row = lax.axis_index("term") * rows + jnp.arange(rows, dtype=jnp.int32)
    index_col = jnp.arange(block, dtype=jnp.int32)
    keep = (index_row[None, :, None] < sector_sizes[:, None, None]) & (
        index_col[None, None, :] < sector_sizes[:, None, None]
    )
    return jnp.where(keep, total, jnp.zeros_like(total))


def solution(mesh):
    placed = (
        P("sector", None, None),
        P("sector"),
        P("term", "sector", None, None),
        P("term", "sector", None, None),
        P("term", "sector"),
        P("term", "sector"),
        P("term", "sector"),
    )
    return jax.shard_map(
        functools.partial(on_device, mesh.shape["term"], mesh.shape["sector"]),
        mesh=mesh, in_specs=placed, out_specs=P("sector", "term", None), check_vma=False,
    )
```

time: 61.3 us -> 52.1 us (0.85)
  Pallas kernels: 54.4 us -> 48.7 us
  other arithmetic: 6.07 us -> 2.55 us
    pallas_call x1, Pallas kernels: 54.4 us -> 48.7 us  [on_device(): pl.pallas_call(functools.partial(kernel, terms, groups), out_shape=jax.Sh...]
    reduce_sum x3 -> x0, other arithmetic: 1.52 us -> none  [the longest x1 0.7 us: on_device(): ends = jnp.sum((tgt[None, :] <= sec[:, None]).astype(jnp.int32), axis=1)]
    add x2 -> x0, other arithmetic: 1.33 us -> none  [the longest x1 0.67 us: on_device(): code = slot + src * 256 + tgt * 65536]
    lt x1 -> x0, other arithmetic: 0.66 us -> none  [on_device(): rank = jnp.sum((key[None, :] < key[:, None]).astype(jnp.int32), axis=1)]
where the time goes in v2:
time: 52.1 us; the launch traced here: 51.9 us
  Pallas kernels  48.7 us (93%)
  other arithmetic  2.55 us (5%)
  between operations  0.69 us (1%)
    pallas_call x1, Pallas kernels, on_device(): pl.pallas_call(functools.partial(kernel, terms, groups), out_shape=jax.Sh...  48.7 us
    select_n x1, other arithmetic, on_device(): return jnp.where(keep, total, jnp.zeros_like(total))  2.4 us

profile of v2, /device:TPU:9, one launch (start us, length us, event | category | flops | bytes accessed | tf_op | source)
XLA Modules:
  0.0 51.9 jit_solution(17394765106486707229)
XLA Ops:
  0.7 0.0 copy-start
  0.7 48.7 %shard_map.73 = f32[16,64,256]{2,1,0:T(8,128)} custom-call(s32[1,1]{1,0:T(1,128)S(6)} %copy.8.live_ref, s32[16]{0:T(128)} %sizes_ref.1, s32[1,48]{1,0:T(1,128)} %bitcast.6, s32[1,48]{1,0:T(1,128)} %bitcast.7, bf16[16,256,256]{2,1,0:T(8,128)(2,1)} %psi_ref.1, bf16[48,256,256]{2,1,0:T(8,128)(2,1)} %bitcast.4, bf16[48,256,256]{2,1,0:T(8,128)(2,1)} %bitcast.5), custom_call_target="tpu_custom_call" | custom-call | tf_op jit(solution)/shard_map/pallas_call | solution.py:278
  49.4 0.0 copy-done
  49.4 0.1 broadcast_compare_fusion
  49.4 0.1 iota_compare_fusion
  49.5 2.4 %and_select_fusion = f32[16,64,256]{2,1,0:T(8,128)} fusion(f32[16,64,256]{2,1,0:T(8,128)} %shard_map.73, pred[16,256]{1,0:T(8,128)(4,1)S(1)} %iota_compare_fusion, pred[16,64]{1,0:T(8,128)(4,1)S(1)} %broadcast_compare_fusion), kind=kLoop, calls=%fused_computation | loop fusion | flops 524288 | bytes 2102272 | tf_op jit(solution)/shard_map/jit(_where)/select_n | solution.py:311
  (1 shorter events, 0.0 us)
Async XLA Ops:
  0.7 48.7 %copy-start = (s32[16]{0:T(128)S(1)}, s32[16]{0:T(128)}, u32[]{:S(2)}) copy-start(s32[16]{0:T(128)} %sizes_ref.1) | copy-start | bytes 196

commit v3 on v2

--- a/solution.py
+++ b/solution.py
@@ -11,7 +11,7 @@
 MESH = pl.DeviceIdType.MESH
 SPLITS = 4
 HALVES = 2
-UNROLL = 4
+UNROLL = 16
 
 
 def kernel(
@@ -64,7 +64,7 @@
         nearby[q] = jnp.where(reach < sizes_ref[q], nearby[q], jnp.zeros((block, block), nearby.dtype))
         return carry
 
-    lax.fori_loop(0, secs, mask, 0)
+    lax.fori_loop(0, secs, mask, 0, unroll=4)
     pl.semaphore_wait(barrier, terms + has_far.astype(jnp.int32))
 
     near_copy = pltpu.make_async_remote_copy(
@@ -219,7 +219,7 @@
                         ).astype(first_out.dtype)
                 return carry
 
-            lax.fori_loop(0, span, give, 0)
+            lax.fori_loop(0, span, give, 0, unroll=True)
             for d in range(1, side):
                 first_copy(half, part, d).start()
 
@@ -243,10 +243,12 @@
                 own[half, part * span + i] = partial_sum(second)
                 return carry
 
-            lax.fori_loop(0, span, pass_on, 0)
+            lax.fori_loop(0, span, pass_on, 0, unroll=True)
             for d in range(1, side):
                 second_copy(half, part, d).start()
 
+    kept_row = lax.broadcasted_iota(jnp.int32, (rows, width), 0) + term * rows
+    kept_col = lax.broadcasted_iota(jnp.int32, (rows, width), 1)
     for half in range(HALVES):
         columns = slice(half * width, (half + 1) * width)
         for part in range(SPLITS):
@@ -257,10 +259,12 @@
                 total = own[half, part * span + i]
                 for d in range(1, side):
                     total = total + second_in[half, part, d - 1, i].astype(jnp.float32)
-                out_ref[part * span + i, :, columns] = total
+                live = sizes_ref[part * span + i]
+                keep = (kept_row < live) & (kept_col < live - half * width)
+                out_ref[part * span + i, :, columns] = jnp.where(keep, total, jnp.zeros_like(total))
                 return carry
 
-            lax.fori_loop(0, span, add, 0)
+            lax.fori_loop(0, span, add, 0, unroll=True)
     for half in range(HALVES):
         for part in range(SPLITS):
             for d in range(1, side):
@@ -275,7 +279,7 @@
     pieces = 2 * (secs // 4)
     dma = pltpu.SemaphoreType.DMA
     smem, vmem, here = (pl.BlockSpec(memory_space=m) for m in (pltpu.SMEM, pltpu.VMEM, pl.ANY))
-    total = pl.pallas_call(
+    return pl.pallas_call(
         functools.partial(kernel, terms, groups),
         out_shape=jax.ShapeDtypeStruct((secs, rows, block), jnp.float32),
         in_specs=[smem, smem, vmem, vmem, here, here, here],
@@ -297,18 +301,12 @@
             *[dma((HALVES, SPLITS, side - 1))] * 4,
         ],
         compiler_params=pltpu.CompilerParams(
-            collective_id=0, has_side_effects=True, vmem_limit_bytes=54 * 1024 * 1024
+            collective_id=0, has_side_effects=True, vmem_limit_bytes=52 * 1024 * 1024
         ),
     )(
         live_count, sector_sizes, target.reshape(1, slots), source.reshape(1, slots),
         psi, left_env[:, 0], right_env[:, 0],
     )
-    index_row = lax.axis_index("term") * rows + jnp.arange(rows, dtype=jnp.int32)
-    index_col = jnp.arange(block, dtype=jnp.int32)
-    keep = (index_row[None, :, None] < sector_sizes[:, None, None]) & (
-        index_col[None, None, :] < sector_sizes[:, None, None]
-    )
-    return jnp.where(keep, total, jnp.zeros_like(total))
 
 
 def solution(mesh):

time: 52.1 us -> 48.4 us (0.929)
  Pallas kernels: 48.7 us -> 44.6 us
  local copies, waits for them, and re-layouts: 0.01 us -> 2.93 us
  other arithmetic: 2.55 us -> 0 us
    pallas_call x1, Pallas kernels: 48.7 us -> 44.6 us  [on_device(): pl.pallas_call(functools.partial(kernel, terms, groups), out_shape=jax.Sh...]
    unnamed x2 -> x7, local copies, waits for them, and re-layouts: 0.01 us -> 2.93 us
    select_n x1 -> x0, other arithmetic: 2.4 us -> none  [on_device(): return jnp.where(keep, total, jnp.zeros_like(total))]
where the time goes in v3:
time: 48.4 us; the launch traced here: 48.2 us
  Pallas kernels  44.6 us (92%)
  local copies, waits for them, and re-layouts  2.93 us (6%)
  between operations  0.67 us (1%)
    pallas_call x1, Pallas kernels, on_device(): pl.pallas_call(functools.partial(kernel, terms, groups), out_shape=jax.Sh...  44.6 us
    unnamed x7, local copies, waits for them, and re-layouts  2.93 us

profile of v3, /device:TPU:9, one launch (start us, length us, event | category | flops | bytes accessed | tf_op | source)
XLA Modules:
  0.0 48.2 jit_solution(17549126137713278935)
XLA Ops:
  0.7 0.0 copy-start
  0.7 0.6 %copy-done = s32[16]{0:T(128)S(1)} copy-done((s32[16]{0:T(128)S(1)}, s32[16]{0:T(128)}, u32[]{:S(2)}) %copy-start) | copy-done | bytes 88
  1.3 0.0 copy-start.1
  1.3 0.7 %copy-done.1 = s32[48,1]{0,1:T(1,128)S(1)} copy-done((s32[48,1]{0,1:T(1,128)S(1)}, s32[48,1]{0,1:T(1,128)}, u32[]{:S(2)}) %copy-start.1) | copy-done | bytes 216
  2.0 0.0 copy-start.2
  2.0 0.7 %copy-done.2 = s32[48,1]{0,1:T(1,128)S(1)} copy-done((s32[48,1]{0,1:T(1,128)S(1)}, s32[48,1]{0,1:T(1,128)}, u32[]{:S(2)}) %copy-start.2) | copy-done | bytes 216
  2.6 44.6 %shard_map.73 = f32[16,64,256]{2,1,0:T(8,128)S(1)} custom-call(s32[1,1]{1,0:T(1,128)S(6)} %copy.9.live_ref, s32[16]{0:T(128)S(1)} %copy-done, s32[1,48]{1,0:T(1,128)S(1)} %bitcast.4, s32[1,48]{1,0:T(1,128)S(1)} %bitcast.5, bf16[16,256,256]{2,1,0:T(8,128)(2,1)} %psi_ref.1, bf16[48,256,256]{2,1,0:T(8,128)(2,1)} %bitcast.6, bf16[48,256,256]{2,1,0:T(8,128)(2,1)} %bitcast.7), custom_call_target="tpu_custom_call" | custom-call | tf_op jit(solution)/shard_map/pallas_call | solution.py:282
  47.2 1.0 %copy.10 = f32[16,64,256]{2,1,0:T(8,128)} copy(f32[16,64,256]{2,1,0:T(8,128)S(1)} %shard_map.73) | data formatting | bytes 2097152
Async XLA Ops:
  0.7 0.7 %copy-start = (s32[16]{0:T(128)S(1)}, s32[16]{0:T(128)}, u32[]{:S(2)}) copy-start(s32[16]{0:T(128)} %sizes_ref.1) | copy-start | bytes 196
  1.3 0.7 %copy-start.1 = (s32[48,1]{0,1:T(1,128)S(1)}, s32[48,1]{0,1:T(1,128)}, u32[]{:S(2)}) copy-start(s32[48,1]{0,1:T(1,128)} %param.11) | copy-start | bytes 580
  2.0 0.7 %copy-start.2 = (s32[48,1]{0,1:T(1,128)S(1)}, s32[48,1]{0,1:T(1,128)}, u32[]{:S(2)}) copy-start(s32[48,1]{0,1:T(1,128)} %param.12) | copy-start | bytes 580

commit v4 on v3

--- a/solution.py
+++ b/solution.py
@@ -10,6 +10,7 @@
 
 MESH = pl.DeviceIdType.MESH
 SPLITS = 4
+DIRECT = 1
 HALVES = 2
 UNROLL = 16
 
@@ -80,6 +81,15 @@
         return 2 * quarter * along_row + odd_here * quarter + k
 
     pieces = 2 * quarter
+    direct = 2 * DIRECT
+    passed = pieces - direct
+
+    def straight_copy(i):
+        q = piece(passed + i, False)
+        return pltpu.make_async_remote_copy(
+            nearby.at[q], nearby.at[2 * secs + q], far_send.at[pieces + i], far_recv.at[pieces + i],
+            device_id={"sector": far}, device_id_type=MESH,
+        )
 
     def far_copy(i):
         q = piece(i, True)
@@ -99,6 +109,8 @@
     def _():
         for i in range(pieces):
             far_copy(i).start()
+        for i in range(direct):
+            straight_copy(i).start()
 
     near_copy.start()
 
@@ -132,7 +144,8 @@
     def _():
         for i in range(pieces):
             far_copy(i).wait_recv()
-            pass_copy(i).start()
+            if i < passed:
+                pass_copy(i).start()
 
     left_load.wait()
     right_load.wait()
@@ -140,11 +153,13 @@
 
     @pl.when(has_far)
     def _():
-        for i in range(pieces):
+        for i in range(passed):
             pass_copy(i, False).wait_recv()
+            pass_copy(i).wait_send()
+        for i in range(direct):
+            straight_copy(i).wait()
         for i in range(pieces):
             far_copy(i).wait_send()
-            pass_copy(i).wait_send()
 
     def multiply(step, carry):
         for u in range(UNROLL):
@@ -297,7 +312,7 @@
             pltpu.VMEM((HALVES, secs, rows, width), jnp.float32),
             pltpu.VMEM((8, 128), jnp.int32),
             pltpu.SMEM((8, 128), jnp.int32),
-            dma((4,)), dma, dma, dma((pieces,)), dma((pieces,)), dma((pieces,)), dma((pieces,)),
+            dma((4,)), dma, dma, dma((pieces + 2 * DIRECT,)), dma((pieces + 2 * DIRECT,)), dma((pieces,)), dma((pieces,)),
             *[dma((HALVES, SPLITS, side - 1))] * 4,
         ],
         compiler_params=pltpu.CompilerParams(

time: 48.4 us -> 46.8 us (0.967)
  Pallas kernels: 44.6 us -> 43.1 us
    pallas_call x1, Pallas kernels: 44.6 us -> 43.1 us  [on_device(): pl.pallas_call(functools.partial(kernel, terms, groups), out_shape=jax.Sh...]
where the time goes in v4:
time: 46.8 us; the launch traced here: 46.7 us
  Pallas kernels  43.1 us (92%)
  local copies, waits for them, and re-layouts  2.93 us (6%)
  between operations  0.67 us (1%)
    pallas_call x1, Pallas kernels, on_device(): pl.pallas_call(functools.partial(kernel, terms, groups), out_shape=jax.Sh...  43.1 us
    unnamed x7, local copies, waits for them, and re-layouts  2.93 us

profile of v4, /device:TPU:9, one launch (start us, length us, event | category | flops | bytes accessed | tf_op | source)
XLA Modules:
  0.0 46.7 jit_solution(13677081108511555839)
XLA Ops:
  0.7 0.0 copy-start
  0.7 0.6 %copy-done = s32[16]{0:T(128)S(1)} copy-done((s32[16]{0:T(128)S(1)}, s32[16]{0:T(128)}, u32[]{:S(2)}) %copy-start) | copy-done | bytes 88
  1.3 0.0 copy-start.1
  1.3 0.7 %copy-done.1 = s32[48,1]{0,1:T(1,128)S(1)} copy-done((s32[48,1]{0,1:T(1,128)S(1)}, s32[48,1]{0,1:T(1,128)}, u32[]{:S(2)}) %copy-start.1) | copy-done | bytes 216
  2.0 0.0 copy-start.2
  2.0 0.7 %copy-done.2 = s32[48,1]{0,1:T(1,128)S(1)} copy-done((s32[48,1]{0,1:T(1,128)S(1)}, s32[48,1]{0,1:T(1,128)}, u32[]{:S(2)}) %copy-start.2) | copy-done | bytes 216
  2.6 43.1 %shard_map.73 = f32[16,64,256]{2,1,0:T(8,128)S(1)} custom-call(s32[1,1]{1,0:T(1,128)S(6)} %copy.9.live_ref, s32[16]{0:T(128)S(1)} %copy-done, s32[1,48]{1,0:T(1,128)S(1)} %bitcast.4, s32[1,48]{1,0:T(1,128)S(1)} %bitcast.5, bf16[16,256,256]{2,1,0:T(8,128)(2,1)} %psi_ref.1, bf16[48,256,256]{2,1,0:T(8,128)(2,1)} %bitcast.6, bf16[48,256,256]{2,1,0:T(8,128)(2,1)} %bitcast.7), custom_call_target="tpu_custom_call" | custom-call | tf_op jit(solution)/shard_map/pallas_call | solution.py:297
  45.7 1.0 %copy.10 = f32[16,64,256]{2,1,0:T(8,128)} copy(f32[16,64,256]{2,1,0:T(8,128)S(1)} %shard_map.73) | data formatting | bytes 2097152
Async XLA Ops:
  0.7 0.7 %copy-start = (s32[16]{0:T(128)S(1)}, s32[16]{0:T(128)}, u32[]{:S(2)}) copy-start(s32[16]{0:T(128)} %sizes_ref.1) | copy-start | bytes 196
  1.3 0.7 %copy-start.1 = (s32[48,1]{0,1:T(1,128)S(1)}, s32[48,1]{0,1:T(1,128)}, u32[]{:S(2)}) copy-start(s32[48,1]{0,1:T(1,128)} %param.11) | copy-start | bytes 580
  2.0 0.7 %copy-start.2 = (s32[48,1]{0,1:T(1,128)S(1)}, s32[48,1]{0,1:T(1,128)}, u32[]{:S(2)}) copy-start(s32[48,1]{0,1:T(1,128)} %param.12) | copy-start | bytes 580
